TPU v7x, 128 devices: a whole 4x4x4 slice. The times are simulated.
128 devices in a mesh: req: 16 (over x, y), mlp: 8 (over z, core).
Axes of the slice: x: 4, y: 4, z: 4, core: 2. Of those that a mesh axis runs over, the one named last changes fastest.
Arguments:
- tokens: bfloat16 [4096, 2048], P(('req', 'mlp')), may hold values from -6 to 6
- cached_states: float32 [256, 8, 256, 512], P('req', 'mlp'), may hold values from -12 to 12
- prompt_lengths: int32 [256], P('req'), may hold values from 1 to 4096, as said below
- accepted: int32 [256], P('req'), may hold values from 1 to 16, as said below
- owner_slot: int32 [256], P('req'), may hold values from 0 to 255, as said below
- w_query: bfloat16 [2048, 2048], P(None, 'mlp'), may hold values from -0.125 to 0.125
- w_key: bfloat16 [2048, 2048], P(None, 'mlp'), may hold values from -0.125 to 0.125
- w_value: bfloat16 [2048, 4096], P(None, 'mlp'), may hold values from -0.125 to 0.125
- w_gate_ret: bfloat16 [2048, 4096], P(None, 'mlp'), may hold values from -0.125 to 0.125
- w_out: bfloat16 [4096, 2048], P('mlp'), may hold values from -0.09375 to 0.09375
- w_gate: bfloat16 [2048, 4096], P('req', 'mlp'), may hold values from -0.125 to 0.125
- w_up: bfloat16 [2048, 4096], P('req', 'mlp'), may hold values from -0.125 to 0.125
- w_down: bfloat16 [4096, 2048], P('mlp', 'req'), may hold values from -0.09375 to 0.09375
Outputs:
- mixed: bfloat16 [4096, 2048], P(('req', 'mlp'))
- new_states: float32 [256, 8, 256, 512], P('req', 'mlp')
Inputs may be any that keep to these rules, and one draw needn't show every extreme that they name: `prompt_lengths`: request r belongs to tenant k = (4 r) // 256, so the four tenants hold consecutive ranges of 64 requests; its prompt length is drawn evenly from 1 to 4^(k + 3). `accepted`: number of leading drafts of request r that are kept, drawn evenly for each request. A permutation of the requests; for request r on req block i = r // 16, owner_slot[r] = j * 16 + i + c with owner block j and 0 <= c < 1, and each pair (j, c) occurs exactly once within a block.
All inputs are finite; a program needn't handle non-finite values.
Results may differ from a plain program's by a relative error of at most 0.017.
Values may be sent and summed in bfloat16 or wider, within the bound.
No kernel may reach another device: no remote copies, remote signals or barrier semaphores. Data moves between devices by JAX's collectives and lax.ppermute only.
A program may use at most 128 MiB of HBM per device.

v0:
```python
import math
import jax
import jax.numpy as jnp
from jax import lax
from jax.sharding import PartitionSpec as P

DRAFT = 16
epsilon = 1e-05


def layer_norm(inputs):
    average = jnp.mean(inputs, axis=-1, keepdims=True)
    centred = inputs - average
    variance = jnp.mean(centred * centred, axis=-1, keepdims=True)
    return centred * lax.rsqrt(variance + epsilon)


def decays(head_count, first_head):
    head_index = jnp.arange(head_count, dtype=jnp.float32) + first_head
    return 1.0 - jnp.exp2(-5.0 - head_index)


def rotate(inputs, positions):
    half_width = inputs.shape[-1] // 2
    frequencies = jnp.exp(
        -math.log(10000.0) * jnp.arange(half_width, dtype=jnp.float32) / half_width
    )
    angles = positions[:, :, None] * frequencies[None, None, :]
    cosine_part = jnp.cos(angles)[:, :, None, :]
    sine_part = jnp.sin(angles)[:, :, None, :]
    front_half = inputs[..., :half_width]
    back_half = inputs[..., half_width:]
    return jnp.concatenate(
        [
            front_half * cosine_part - back_half * sine_part,
            front_half * sine_part + back_half * cosine_part,
        ],
        axis=-1,
    )


def state_weights(states, accepted, gammas, draft_count):
    draft_pos = jnp.arange(draft_count, dtype=jnp.float32)
    accepted_f = accepted.astype(jnp.float32)
    exponent = accepted_f[:, None, None] - 1.0 - draft_pos[None, None, :]
    draft_weights = jnp.where(
        exponent >= 0, jnp.power(gammas[None, :, None], jnp.maximum(exponent, 0.0)), 0.0
    )
    old_part = jnp.power(gammas[None, :], accepted_f[:, None])[:, :, None, None] * states
    return (old_part, draft_weights)


def fold_update(key_rows, values, draft_weights):
    scaled = key_rows.astype(jnp.float32) * jnp.transpose(draft_weights, (0, 2, 1))[..., None]
    return jnp.einsum(
        "rshd,rshv->rhdv", scaled, values.astype(jnp.float32), precision=lax.Precision.HIGHEST
    )


def retain_outputs(queries, key_rows, values, states, gammas):
    draft_count = queries.shape[1]
    draft_pos = jnp.arange(draft_count, dtype=jnp.float32)
    distance = draft_pos[:, None] - draft_pos[None, :]
    decay_mask = jnp.where(
        distance[None] >= 0, jnp.power(gammas[:, None, None], jnp.maximum(distance, 0.0)[None]), 0.0
    )
    scores = jnp.einsum("rthd,rshd->rhts", queries, key_rows, preferred_element_type=jnp.float32)
    weights = (scores * decay_mask[None]).astype(jnp.bfloat16)
    within = jnp.einsum("rhts,rshv->rthv", weights, values, preferred_element_type=jnp.float32)
    carried = jnp.einsum(
        "rthd,rhdv->rthv", queries.astype(jnp.float32), states, precision=lax.Precision.HIGHEST
    )
    carried = carried * jnp.power(gammas[None, None, :, None], draft_pos[None, :, None, None] + 1.0)
    return within + carried


def per_device(
    tokens,
    cached_states,
    prompt_lengths,
    accepted,
    owner_slot,
    w_query,
    w_key,
    w_value,
    w_gate_ret,
    w_out,
    w_gate,
    w_up,
    w_down,
):
    requests = cached_states.shape[0]
    heads_here = cached_states.shape[1]
    key_width = cached_states.shape[2]
    value_width = cached_states.shape[3]
    draft_count = DRAFT
    per_peer = requests // lax.axis_size("req")
    first_head = (lax.axis_index("mlp") * heads_here).astype(jnp.float32)
    gammas = decays(heads_here, first_head)
    target_pos = owner_slot // requests * per_peer + owner_slot % per_peer
    local_ids = jnp.arange(requests, dtype=jnp.int32)
    send_order = jnp.sum(
        jnp.where(target_pos[None, :] == local_ids[:, None], local_ids[None, :], 0), axis=1
    )
    old_part, draft_weights = state_weights(cached_states, accepted, gammas, draft_count)
    group_rows = lax.all_gather(tokens, "mlp", axis=0, tiled=True)
    row_count = group_rows.shape[0]
    normed = layer_norm(group_rows.astype(jnp.float32)).astype(jnp.bfloat16)
    queries = jnp.dot(normed, w_query, preferred_element_type=jnp.float32).reshape(
        requests, draft_count, heads_here, key_width
    )
    key_rows = (
        jnp.dot(normed, w_key, preferred_element_type=jnp.float32) * (1.0 / math.sqrt(key_width))
    ).reshape(requests, draft_count, heads_here, key_width)
    values = (
        jnp.dot(normed, w_value, preferred_element_type=jnp.float32)
        .astype(jnp.bfloat16)
        .reshape(requests, draft_count, heads_here, value_width)
    )
    gate_ret = jnp.dot(normed, w_gate_ret, preferred_element_type=jnp.float32).reshape(
        requests, draft_count, heads_here, value_width
    )
    positions = (
        prompt_lengths[:, None] + jnp.arange(draft_count, dtype=jnp.int32)[None, :]
    ).astype(jnp.float32)
    rotated_q = rotate(queries, positions).astype(jnp.bfloat16)
    rotated_k = rotate(key_rows, positions).astype(jnp.bfloat16)
    fresh = old_part + fold_update(rotated_k, values, draft_weights)
    new_states = lax.all_to_all(
        jnp.take(fresh, send_order, axis=0).astype(jnp.bfloat16),
        "req",
        split_axis=0,
        concat_axis=0,
        tiled=True,
    ).astype(jnp.float32)
    outputs = retain_outputs(rotated_q, rotated_k, values, cached_states, gammas)
    joined = (
        (layer_norm(outputs) * jax.nn.silu(gate_ret))
        .astype(jnp.bfloat16)
        .reshape(row_count, heads_here * value_width)
    )
    partials = jnp.dot(joined, w_out, preferred_element_type=jnp.float32)
    share = tokens.shape[0]
    summed = lax.psum(partials.astype(jnp.bfloat16), "mlp").astype(jnp.float32)
    residual = group_rows.astype(jnp.float32) + summed
    hidden_in = layer_norm(residual).astype(jnp.bfloat16)
    residual_share = lax.dynamic_slice_in_dim(residual, lax.axis_index("mlp") * share, share, 0)
    gate_sum = jnp.dot(
        hidden_in,
        lax.all_gather(w_gate, "req", axis=0, tiled=True),
        preferred_element_type=jnp.float32,
    )
    up_sum = jnp.dot(
        hidden_in,
        lax.all_gather(w_up, "req", axis=0, tiled=True),
        preferred_element_type=jnp.float32,
    )
    hidden = (jax.nn.silu(gate_sum) * up_sum).astype(jnp.bfloat16)
    down_terms = jnp.dot(
        hidden,
        lax.all_gather(w_down, "req", axis=1, tiled=True),
        preferred_element_type=jnp.float32,
    )
    mixed = (
        residual_share
        + lax.psum_scatter(
            down_terms.astype(jnp.bfloat16), "mlp", scatter_dimension=0, tiled=True
        ).astype(jnp.float32)
    ).astype(jnp.bfloat16)
    return (mixed, new_states)


def solution(mesh):
    return jax.shard_map(
        per_device,
        mesh=mesh,
        in_specs=(
            P(("req", "mlp"), None),
            P("req", "mlp", None, None),
            P("req"),
            P("req"),
            P("req"),
            P(None, "mlp"),
            P(None, "mlp"),
            P(None, "mlp"),
            P(None, "mlp"),
            P("mlp", None),
            P("req", "mlp"),
            P("req", "mlp"),
            P("mlp", "req"),
        ),
        out_specs=(P(("req", "mlp"), None), P("req", "mlp", None, None)),
        check_vma=False,
    )
```

profile of v0, /device:TPU:0, one launch (start us, length us, event | category | flops | bytes accessed | tf_op | source)
XLA Modules:
  0.0 292.6 jit_solution(9923239641830720972)
XLA Ops:
  8.1 0.7 all-gather.5.cloned.1.call-update
  8.9 1.3 convert_add_fusion.1
  10.2 0.7 add_convert_fusion.1
  10.9 0.7 power_select_fusion
  11.6 25.0 %all-gather.5.cloned.1.call-done = bf16[256,2048]{1,0:T(8,128)(2,1)} async-done(((bf16[32,2048]{1,0:T(8,128)(2,1)}), bf16[256,2048]{1,0:T(8,128)(2,1)}) %all-gather.5.cloned.1.call-update) | async-done | bytes 1048592 | tf_op jit(solution)/shard_map/all_gather | solution.py:106
  36.6 1.6 convert_reduce_fusion
  38.3 2.0 fusion.7
  40.3 1.7 fusion.62
  42.0 2.0 convolution_multiply_fusion.1
  44.0 0.6 fusion.46
  44.7 0.6 copy-done.5
  45.3 3.7 %fusion.14 = f32[16,1,512,16]{2,3,0,1:T(8,128)} fusion(f32[16,1,256,512]{3,2,1,0:T(8,128)S(1)} %copy-done.1, f32[16]{0:T(128)S(1)} %add_power_fusion, bf16[16,16,128]{2,1,0:T(8,128)(2,1)S(1)} %get-tuple-element.10, bf16[16,16,128]{2,1,0:T(8,128)(2,1)S(1)} %get-tuple-element.11), kind=kOutput, calls=%fused_computation.25 | convolution fusion | flops 403046400 | bytes 9044032 | tf_op jit(solution)/shard_map/rthd,rhdv->rthv/dot_general | solution.py:70
  49.0 0.8 convolution_convert_fusion.2
  49.7 2.2 fusion.65
  52.0 1.2 multiply_reduce_fusion.1
  53.2 2.4 fusion.59
  56.0 1.7 convolution_convert_fusion.1
  58.3 0.5 all-gather.9.cloned.1.call-update
  60.1 8.5 %fusion.1 = bf16[16,256,512]{2,1,0:T(8,128)(2,1)} fusion(f32[16,1,256,512]{3,2,1,0:T(8,128)} %param.14, f32[16]{0:T(128)S(1)} %copy-done.9, bf16[16,16,512]{2,1,0:T(8,128)(2,1)S(1)} %bitcast.68, f32[16,16]{1,0:T(8,128)S(1)} %copy-done.7, bf16[16,16,128]{2,1,0:T(8,128)(2,1)S(1)} %get-tuple-element.7, bf16[16,16,128]{2,1,0:T(8,128)(2,1)S(1)} %get-tuple-element.6), kind=kOutput, calls=%fused_computation.4 | convolution fusion | flops 409272320 | bytes 12977216 | tf_op jit(solution)/shard_map/rshd,rshv->rhdv/dot_general | solution.py:55
  68.7 5.1 %gather_fusion = bf16[16,256,512]{2,1,0:T(8,128)(2,1)} fusion(bf16[16,256,512]{2,1,0:T(8,128)(2,1)} %fusion.1, s32[1024]{0:T(1024)S(1)} %pad_clamp_fusion), kind=kCustom, calls=%fused_computation | custom fusion | bytes 8388672 | tf_op jit(solution)/shard_map/jit(_take)/gather | solution.py:130
  73.7 5.5 %fusion.4 = bf16[16,1,256,512]{3,2,1,0:T(8,128)(2,1)} fusion(bf16[16,256,512]{2,1,0:T(8,128)(2,1)} %gather_fusion, pred[16]{0:T(512)(128)(4,1)S(1)} %copy-done.11), kind=kLoop, calls=%fused_computation.8 | loop fusion | flops 2097152 | bytes 8388624 | tf_op jit(solution)/shard_map/convert_element_type | solution.py:130
  79.2 6.9 %all-to-all-start = ((bf16[16,1,256,512]{3,2,1,0:T(8,128)(2,1)}), bf16[16,1,256,512]{3,2,1,0:T(8,128)(2,1)}, u32[]{:S(2)}, u32[]{:S(2)}) async-start(bf16[16,1,256,512]{3,2,1,0:T(8,128)(2,1)} %fusion.4), calls=%async_computation.1 | async-start | bytes 8388608 | tf_op jit(solution)/shard_map/all_to_all | solution.py:129
  86.3 35.1 %all-reduce.2.cloned.1.call-done = bf16[256,2048]{1,0:T(8,128)(2,1)} async-done(((bf16[256,2048]{1,0:T(8,128)(2,1)}), bf16[256,2048]{1,0:T(8,128)(2,1)}) %all-reduce.2.cloned.1.call-update) | async-done | bytes 1048592 | tf_op jit(solution)/shard_map/psum | solution.py:144
  121.4 2.9 convert_add_fusion
  124.8 18.6 %all-gather.7.cloned.1.call-done = bf16[2048,512]{1,0:T(8,128)(2,1)} async-done(((bf16[128,512]{1,0:T(8,128)(2,1)}), bf16[2048,512]{1,0:T(8,128)(2,1)}) %all-gather.7.cloned.1.call-update) | async-done | bytes 2097168 | tf_op jit(solution)/shard_map/all_gather | solution.py:150
  143.5 3.5 %fusion.58 = f32[256,512]{1,0:T(8,128)} fusion(bf16[2048,512]{1,0:T(8,128)(2,1)} %all-gather.7.cloned.1.call-done, f32[256]{0:T(256)S(1)} %add_rsqrt_fusion.1, f32[256]{0:T(256)S(1)} %broadcast_multiply_fusion.1, bf16[256,2048]{1,0:T(8,128)(2,1)} %all-reduce.2.cloned.1.call-done, bf16[256,2048]{1,0:T(8,128)(2,1)S(1)} %copy-done.2), kind=kOutput, calls=%fused_computation.101 | convolution fusion | flops 540016640 | bytes 4720640 | tf_op jit(solution)/shard_map/dot_general | solution.py:148
  147.0 51.2 %all-gather.9.cloned.1.call-done = bf16[2048,512]{1,0:T(8,128)(2,1)} async-done(((bf16[128,512]{1,0:T(8,128)(2,1)}), bf16[2048,512]{1,0:T(8,128)(2,1)}) %all-gather.9.cloned.1.call-update) | async-done | bytes 2097168 | tf_op jit(solution)/shard_map/all_gather | solution.py:155
  198.2 48.6 %all-gather.11.cloned.1.call-done = bf16[512,2048]{1,0:T(8,128)(2,1)} async-done(((bf16[512,128]{1,0:T(8,128)(2,1)}), bf16[512,2048]{1,0:T(8,128)(2,1)}) %all-gather.11.cloned.1.call-update) | async-done | bytes 2097168 | tf_op jit(solution)/shard_map/all_gather | solution.py:161
  246.8 5.2 %convolution_convert_fusion = bf16[256,2048]{1,0:T(8,128)(2,1)} fusion(bf16[512,2048]{1,0:T(8,128)(2,1)} %all-gather.11.cloned.1.call-done, bf16[2048,512]{1,0:T(8,128)(2,1)} %all-gather.9.cloned.1.call-done, f32[256,512]{1,0:T(8,128)} %fusion.58, f32[256]{0:T(256)S(1)} %add_rsqrt_fusion.1, f32[256]{0:T(256)S(1)} %broadcast_multiply_fusion.1, ...), kind=kOutput, calls=%fused_computation.12 | convolution fusion | flops 1078198272 | bytes 7866368 | tf_op jit(solution)/shard_map/dot_general | solution.py:159
  252.0 6.7 %convert_element_type.101 = f32[16,1,256,512]{3,2,1,0:T(8,128)} convert(bf16[16,1,256,512]{3,2,1,0:T(8,128)(2,1)} %all-to-all-done) | non-fusion elementwise | flops 2097152 | bytes 12582912 | tf_op jit(solution)/shard_map/convert_element_type | solution.py:135
  258.7 24.9 %reduce-scatter.2.cloned.1.call-done = bf16[32,2048]{1,0:T(8,128)(2,1)} async-done(((bf16[256,2048]{1,0:T(8,128)(2,1)}), bf16[32,2048]{1,0:T(8,128)(2,1)}) %reduce-scatter.2.cloned.1.call-update) | async-done | bytes 131088 | tf_op jit(solution)/shard_map/reduce_scatter | solution.py:166
  283.6 1.7 add_convert_fusion
  (55 shorter events, 3.1 us)
Async XLA Ops:
  8.0 47.9 %copy-start = (bf16[512,2048]{1,0:T(8,128)(2,1)S(1)}, bf16[512,2048]{1,0:T(8,128)(2,1)}, u32[]{:S(2)}) copy-start(bf16[512,2048]{1,0:T(8,128)(2,1)} %param.22) | copy-start | bytes 6291460
  8.0 32.2 %copy-start.13 = (bf16[2048,256]{1,0:T(8,128)(2,1)S(1)}, bf16[2048,256]{1,0:T(8,128)(2,1)}, u32[]{:S(2)}) copy-start(bf16[2048,256]{1,0:T(8,128)(2,1)} %param.18) | copy-start | bytes 3145732
  8.0 28.6 %all-gather.5.cloned.1.call-start = ((), (), s32[]{:S(2)}) async-start(), calls=%async_computation.2 | async-start | bytes 1179648 | tf_op jit(solution)/shard_map/all_gather | solution.py:106
  8.8 112.6 %all-reduce.2.cloned.1.call-start = ((), (), s32[]{:S(2)}) async-start(), calls=%async_computation.3 | async-start | bytes 2097152 | tf_op jit(solution)/shard_map/psum | solution.py:144
  36.6 8.6 %copy-start.1 = (f32[16,1,256,512]{3,2,1,0:T(8,128)S(1)}, f32[16,1,256,512]{3,2,1,0:T(8,128)}, u32[]{:S(2)}) copy-start(f32[16,1,256,512]{3,2,1,0:T(8,128)} %param.14) | copy-start | bytes 25165828
  38.3 10.7 %copy-start.8 = (f32[256]{0:T(256)}, f32[256]{0:T(256)S(1)}, u32[]{:S(2)}) copy-start(f32[256]{0:T(256)S(1)} %broadcast_multiply_fusion.2) | copy-start | bytes 3076
  40.2 8.7 %copy-start.10 = (f32[256]{0:T(256)}, f32[256]{0:T(256)S(1)}, u32[]{:S(2)}) copy-start(f32[256]{0:T(256)S(1)} %add_rsqrt_fusion.2) | copy-start | bytes 3076
  44.6 0.6 copy-start.5
  44.6 0.6 copy-start.6
  45.3 3.7 %copy-start.2 = (bf16[256,2048]{1,0:T(8,128)(2,1)S(1)}, bf16[256,2048]{1,0:T(8,128)(2,1)}, u32[]{:S(2)}) copy-start(bf16[256,2048]{1,0:T(8,128)(2,1)} %all-gather.5.cloned.1.call-done) | copy-start | bytes 3145732
  45.3 3.7 %copy-start.12 = (bf16[2048,512]{1,0:T(8,128)(2,1)S(1)}, bf16[2048,512]{1,0:T(8,128)(2,1)}, u32[]{:S(2)}) copy-start(bf16[2048,512]{1,0:T(8,128)(2,1)} %param.20) | copy-start | bytes 6291460
  53.2 2.4 copy-start.3
  55.9 3.5 %copy-start.14 = (s32[16]{0:T(128)S(1)}, s32[16]{0:T(128)}, u32[]{:S(2)}) copy-start(s32[16]{0:T(128)} %param.17) | copy-start | bytes 196
  55.9 4.2 %copy-start.7 = (f32[16,16]{1,0:T(8,128)S(1)}, f32[16,16]{1,0:T(8,128)}, u32[]{:S(2)}) copy-start(f32[16,16]{1,0:T(8,128)} %get-tuple-element.16) | copy-start | bytes 3076
  55.9 4.2 %copy-start.9 = (f32[16]{0:T(128)S(1)}, f32[16]{0:T(128)}, u32[]{:S(2)}) copy-start(f32[16]{0:T(128)} %get-tuple-element.13) | copy-start | bytes 196
  57.7 85.8 %all-gather.7.cloned.1.call-start = ((), (), s32[]{:S(2)}) async-start(), calls=%async_computation.4 | async-start | bytes 2228224 | tf_op jit(solution)/shard_map/all_gather | solution.py:150
  58.3 139.9 %all-gather.9.cloned.1.call-start = ((), (), s32[]{:S(2)}) async-start(), calls=%async_computation.5 | async-start | bytes 2228224 | tf_op jit(solution)/shard_map/all_gather | solution.py:155
  58.9 187.9 %all-gather.11.cloned.1.call-start = ((), (), s32[]{:S(2)}) async-start(), calls=%async_computation.6 | async-start | bytes 2228224 | tf_op jit(solution)/shard_map/all_gather | solution.py:161
  68.7 5.1 %copy-start.11 = (pred[16]{0:T(512)(128)(4,1)S(1)}, pred[16]{0:T(512)(128)(4,1)}, u32[]{:S(2)}) copy-start(pred[16]{0:T(512)(128)(4,1)} %compare_and_fusion) | copy-start | bytes 52
  79.2 172.8 %all-to-all-start = ((bf16[16,1,256,512]{3,2,1,0:T(8,128)(2,1)}), bf16[16,1,256,512]{3,2,1,0:T(8,128)(2,1)}, u32[]{:S(2)}, u32[]{:S(2)}) async-start(bf16[16,1,256,512]{3,2,1,0:T(8,128)(2,1)} %fusion.4), calls=%async_computation.1 | async-start | bytes 8388608 | tf_op jit(solution)/shard_map/all_to_all | solution.py:129
  86.1 197.5 %reduce-scatter.2.cloned.1.call-start = ((), (), s32[]{:S(2)}) async-start(), calls=%async_computation.7 | async-start | bytes 1179648 | tf_op jit(solution)/shard_map/reduce_scatter | solution.py:166
  121.4 2.9 copy-start.4
Sparse Core Ops, SparseCore 0:
  10.6 26.0 all-gather.4
  57.8 63.5 all-reduce.1
  252.1 31.4 reduce-scatter.1
Sparse Core Ops, SparseCore 1:
  60.3 83.1 all-gather.6
  145.5 52.7 all-gather.8
  200.2 46.5 all-gather.10
where the time goes:
time: 293 us
  waiting for transfers between devices  206 us (70%)
  matrix products  31.8 us (11%)
  other arithmetic  26.4 us (9%)
  between operations  15.7 us (5%)
  starting transfers between devices  7.29 us (2%)
  local copies, waits for them, and re-layouts  5.76 us (2%)
    all_gather x1, waiting for transfers between devices, per_device(): lax.all_gather(w_up, 'req', axis=0, tiled=True)  51.2 us
    all_gather x1, waiting for transfers between devices, per_device(): lax.all_gather(w_down, 'req', axis=1, tiled=True)  48.6 us
    psum x1, waiting for transfers between devices, per_device(): summed = lax.psum(partials.astype(jnp.bfloat16), 'mlp').astype(jnp.float32)  35.1 us
    all_gather x1, waiting for transfers between devices, per_device(): group_rows = lax.all_gather(tokens, 'mlp', axis=0, tiled=True)  25 us
    reduce_scatter x1, waiting for transfers between devices, per_device(): lax.psum_scatter(down_terms.astype(jnp.bfloat16), 'mlp', scatter_dimensio...  24.9 us
    all_gather x1, waiting for transfers between devices, per_device(): lax.all_gather(w_gate, 'req', axis=0, tiled=True)  18.6 us
    dot_general x1, matrix products, fold_update(): jnp.einsum('rshd,rshv->rhdv', scaled, values.astype(jnp.float32), precisi...  8.54 us
    all_to_all x1, starting transfers between devices, per_device(): lax.all_to_all(jnp.take(fresh, send_order, axis=0).astype(jnp.bfloat16),...  6.87 us
  transfers between devices with their start and end apart: 7, of which 6 were waited for; matrix products, arithmetic and copies ran while one was open for 14% of the time, Pallas kernels for 0%

commit v1 on v0

--- a/solution.py
+++ b/solution.py
@@ -103,7 +103,9 @@
         jnp.where(target_pos[None, :] == local_ids[:, None], local_ids[None, :], 0), axis=1
     )
     old_part, draft_weights = state_weights(cached_states, accepted, gammas, draft_count)
-    group_rows = lax.all_gather(tokens, "mlp", axis=0, tiled=True)
+    group_rows = jnp.concatenate(
+        lax.all_to_all(jnp.stack([tokens] * lax.axis_size("mlp")), "mlp", 0, 0), axis=0
+    )
     row_count = group_rows.shape[0]
     normed = layer_norm(group_rows.astype(jnp.float32)).astype(jnp.bfloat16)
     queries = jnp.dot(normed, w_query, preferred_element_type=jnp.float32).reshape(

time: 293 us -> 284 us (0.969)
  waiting for transfers between devices: 206 us -> 190 us
  starting transfers between devices: 7.29 us -> 12.8 us
    all_gather x1 -> x0, waiting for transfers between devices: 25 us -> none  [per_device(): group_rows = lax.all_gather(tokens, 'mlp', axis=0, tiled=True)]
    all_to_all x0 -> x1, waiting for transfers between devices: none -> 13.5 us  [per_device(): lax.all_to_all(jnp.stack([tokens] * lax.axis_size('mlp')), 'mlp', 0, 0)]
    all_gather x1, waiting for transfers between devices: 51.2 us -> 43.3 us  [per_device(): lax.all_gather(w_up, 'req', axis=0, tiled=True)]
    all_to_all x0 -> x1, starting transfers between devices: none -> 5.4 us  [per_device(): lax.all_to_all(jnp.stack([tokens] * lax.axis_size('mlp')), 'mlp', 0, 0)]
    all_gather x1, waiting for transfers between devices: 18.6 us -> 23.5 us  [per_device(): lax.all_gather(w_gate, 'req', axis=0, tiled=True)]
  transfers between devices with their start and end apart: 7 -> 7, of which waited for: 6 -> 6; matrix products, arithmetic and copies ran while one was open for 14% -> 15% of each run, Pallas kernels for 0% -> 0%
where the time goes in v1:
time: 284 us; the launch traced here: 283 us
  waiting for transfers between devices  190 us (67%)
  matrix products  30.7 us (11%)
  other arithmetic  26.2 us (9%)
  between operations  16 us (6%)
  starting transfers between devices  12.8 us (5%)
  local copies, waits for them, and re-layouts  7.79 us (3%)
    all_gather x1, waiting for transfers between devices, per_device(): lax.all_gather(w_down, 'req', axis=1, tiled=True)  48.6 us
    all_gather x1, waiting for transfers between devices, per_device(): lax.all_gather(w_up, 'req', axis=0, tiled=True)  43.3 us
    psum x1, waiting for transfers between devices, per_device(): summed = lax.psum(partials.astype(jnp.bfloat16), 'mlp').astype(jnp.float32)  34.4 us
    reduce_scatter x1, waiting for transfers between devices, per_device(): lax.psum_scatter(down_terms.astype(jnp.bfloat16), 'mlp', scatter_dimensio...  24.9 us
    all_gather x1, waiting for transfers between devices, per_device(): lax.all_gather(w_gate, 'req', axis=0, tiled=True)  23.5 us
    all_to_all x1, waiting for transfers between devices, per_device(): lax.all_to_all(jnp.stack([tokens] * lax.axis_size('mlp')), 'mlp', 0, 0)  13.5 us
    dot_general x1, matrix products, fold_update(): jnp.einsum('rshd,rshv->rhdv', scaled, values.astype(jnp.float32), precisi...  8.54 us
    all_to_all x1, starting transfers between devices, per_device(): lax.all_to_all(jnp.take(fresh, send_order, axis=0).astype(jnp.bfloat16),...  7.05 us
  transfers between devices with their start and end apart: 7, of which 6 were waited for; matrix products, arithmetic and copies ran while one was open for 15% of the time, Pallas kernels for 0%

profile of v1, /device:TPU:0, one launch (start us, length us, event | category | flops | bytes accessed | tf_op | source)
XLA Modules:
  0.0 283.3 jit_solution(13911037226075771470)
XLA Ops:
  8.0 2.1 stack.2
  10.2 5.4 %all-to-all-start = ((bf16[8,32,2048]{2,1,0:T(8,128)(2,1)}), bf16[8,32,2048]{2,1,0:T(8,128)(2,1)S(1)}, u32[]{:S(2)}, u32[]{:S(2)}) async-start(bf16[8,32,2048]{2,1,0:T(8,128)(2,1)} %stack.2), calls=%async_computation | async-start | bytes 2097152 | tf_op jit(solution)/shard_map/all_to_all | solution.py:107
  15.7 0.5 multiply_exponential_fusion
  16.2 0.6 add_power_fusion
  16.7 0.6 convert_add_fusion
  17.4 0.7 power_select_fusion
  18.1 13.5 %all-to-all-done = bf16[8,32,2048]{2,1,0:T(8,128)(2,1)S(1)} async-done(((bf16[8,32,2048]{2,1,0:T(8,128)(2,1)}), bf16[8,32,2048]{2,1,0:T(8,128)(2,1)S(1)}, u32[]{:S(2)}, u32[]{:S(2)}) %all-to-all-start) | async-done | bytes 1048608 | tf_op jit(solution)/shard_map/all_to_all | solution.py:107
  32.9 1.8 convolution_multiply_fusion.1
  34.7 2.5 convolution_convert_fusion.2
  37.2 1.5 fusion.63
  39.4 0.6 fusion.49
  40.1 3.7 %fusion.14 = f32[16,1,512,16]{2,3,0,1:T(8,128)} fusion(f32[16,1,256,512]{3,2,1,0:T(8,128)S(1)} %bitcast.92, f32[16]{0:T(128)S(1)} %copy-done.7, bf16[16,16,128]{2,1,0:T(8,128)(2,1)S(1)} %get-tuple-element.10, bf16[16,16,128]{2,1,0:T(8,128)(2,1)S(1)} %get-tuple-element.11), kind=kOutput, calls=%fused_computation.27 | convolution fusion | flops 403046400 | bytes 9044032 | tf_op jit(solution)/shard_map/rthd,rhdv->rthv/dot_general | solution.py:70
  43.7 2.2 fusion.61
  46.0 1.2 multiply_reduce_fusion.1
  47.2 1.4 multiply_convert_fusion.3
  48.7 1.7 convolution_convert_fusion.1
  51.1 0.5 all-gather.6.cloned.1.call-update
  52.9 8.5 %fusion.1 = bf16[16,256,512]{2,1,0:T(8,128)(2,1)} fusion(f32[16,1,256,512]{3,2,1,0:T(8,128)} %param.14, f32[16]{0:T(128)S(1)} %copy-done.6, bf16[16,16,512]{2,1,0:T(8,128)(2,1)S(1)} %bitcast.94, f32[16,16]{1,0:T(8,128)S(1)} %copy-done.5, bf16[16,16,128]{2,1,0:T(8,128)(2,1)S(1)} %get-tuple-element.7, bf16[16,16,128]{2,1,0:T(8,128)(2,1)S(1)} %get-tuple-element.6), kind=kOutput, calls=%fused_computation.4 | convolution fusion | flops 409272320 | bytes 12977216 | tf_op jit(solution)/shard_map/rshd,rshv->rhdv/dot_general | solution.py:55
  61.4 5.1 %gather_fusion = bf16[16,256,512]{2,1,0:T(8,128)(2,1)} fusion(bf16[16,256,512]{2,1,0:T(8,128)(2,1)} %fusion.1, s32[1024]{0:T(1024)S(1)} %pad_clamp_fusion), kind=kCustom, calls=%fused_computation | custom fusion | bytes 8388672 | tf_op jit(solution)/shard_map/jit(_take)/gather | solution.py:132
  66.5 5.5 %fusion.4 = bf16[16,1,256,512]{3,2,1,0:T(8,128)(2,1)} fusion(bf16[16,256,512]{2,1,0:T(8,128)(2,1)} %gather_fusion, pred[16]{0:T(512)(128)(4,1)S(1)} %copy-done.8), kind=kLoop, calls=%fused_computation.8 | loop fusion | flops 2097152 | bytes 8388624 | tf_op jit(solution)/shard_map/convert_element_type | solution.py:132
  72.1 7.1 %all-to-all-start.1 = ((bf16[16,1,256,512]{3,2,1,0:T(8,128)(2,1)}), bf16[16,1,256,512]{3,2,1,0:T(8,128)(2,1)}, u32[]{:S(2)}, u32[]{:S(2)}) async-start(bf16[16,1,256,512]{3,2,1,0:T(8,128)(2,1)} %fusion.4), calls=%async_computation.2 | async-start | bytes 8388608 | tf_op jit(solution)/shard_map/all_to_all | solution.py:131
  79.3 34.4 %all-reduce.2.cloned.1.call-done = bf16[256,2048]{1,0:T(8,128)(2,1)} async-done(((bf16[256,2048]{1,0:T(8,128)(2,1)}), bf16[256,2048]{1,0:T(8,128)(2,1)}) %all-reduce.2.cloned.1.call-update) | async-done | bytes 1048592 | tf_op jit(solution)/shard_map/psum | solution.py:146
  113.8 2.9 %bitcast_add_fusion.1 = (f32[256,2048]{1,0:T(8,128)}, f32[256]{0:T(256)S(1)}) fusion(bf16[8,32,2048]{2,1,0:T(8,128)(2,1)S(1)} %all-to-all-done, bf16[256,2048]{1,0:T(8,128)(2,1)} %all-reduce.2.cloned.1.call-done), kind=kLoop, calls=%fused_computation.11 | loop fusion | flops 2096896 | bytes 4195328 | tf_op jit(solution)/shard_map/add | solution.py:147
  117.2 1.4 multiply_convert_fusion
  118.7 23.5 %all-gather.4.cloned.1.call-done = bf16[2048,512]{1,0:T(8,128)(2,1)} async-done(((bf16[128,512]{1,0:T(8,128)(2,1)}), bf16[2048,512]{1,0:T(8,128)(2,1)}) %all-gather.4.cloned.1.call-update) | async-done | bytes 2097168 | tf_op jit(solution)/shard_map/all_gather | solution.py:152
  142.2 3.4 %fusion.64 = f32[256,512]{1,0:T(8,128)} fusion(bf16[256,2048]{1,0:T(8,128)(2,1)} %multiply_convert_fusion, bf16[2048,512]{1,0:T(8,128)(2,1)} %all-gather.4.cloned.1.call-done), kind=kOutput, calls=%fused_computation.110 | convolution fusion | flops 536870912 | bytes 3670016 | tf_op jit(solution)/shard_map/dot_general | solution.py:150
  145.6 43.3 %all-gather.6.cloned.1.call-done = bf16[2048,512]{1,0:T(8,128)(2,1)} async-done(((bf16[128,512]{1,0:T(8,128)(2,1)}), bf16[2048,512]{1,0:T(8,128)(2,1)}) %all-gather.6.cloned.1.call-update) | async-done | bytes 2097168 | tf_op jit(solution)/shard_map/all_gather | solution.py:157
  188.9 48.6 %all-gather.8.cloned.1.call-done = bf16[512,2048]{1,0:T(8,128)(2,1)} async-done(((bf16[512,128]{1,0:T(8,128)(2,1)}), bf16[512,2048]{1,0:T(8,128)(2,1)}) %all-gather.8.cloned.1.call-update) | async-done | bytes 2097168 | tf_op jit(solution)/shard_map/all_gather | solution.py:163
  237.5 4.8 %convolution_convert_fusion = bf16[256,2048]{1,0:T(8,128)(2,1)} fusion(bf16[512,2048]{1,0:T(8,128)(2,1)} %all-gather.8.cloned.1.call-done, bf16[256,2048]{1,0:T(8,128)(2,1)S(1)} %copy-done.2, bf16[2048,512]{1,0:T(8,128)(2,1)} %all-gather.6.cloned.1.call-done, f32[256,512]{1,0:T(8,128)} %fusion.64), kind=kOutput, calls=%fused_computation.9 | convolution fusion | flops 1075052544 | bytes 6815744 | tf_op jit(solution)/shard_map/dot_general | solution.py:161
  242.3 6.7 %convert_element_type.130 = f32[16,1,256,512]{3,2,1,0:T(8,128)} convert(bf16[16,1,256,512]{3,2,1,0:T(8,128)(2,1)} %all-to-all-done.1) | non-fusion elementwise | flops 2097152 | bytes 12582912 | tf_op jit(solution)/shard_map/convert_element_type | solution.py:137
  249.1 24.9 %reduce-scatter.2.cloned.1.call-done = bf16[32,2048]{1,0:T(8,128)(2,1)} async-done(((bf16[256,2048]{1,0:T(8,128)(2,1)}), bf16[32,2048]{1,0:T(8,128)(2,1)}) %reduce-scatter.2.cloned.1.call-update) | async-done | bytes 131088 | tf_op jit(solution)/shard_map/reduce_scatter | solution.py:168
  274.0 1.7 add_convert_fusion
  (66 shorter events, 4.7 us)
Async XLA Ops:
  8.0 40.7 %copy-start = (bf16[512,2048]{1,0:T(8,128)(2,1)S(1)}, bf16[512,2048]{1,0:T(8,128)(2,1)}, u32[]{:S(2)}) copy-start(bf16[512,2048]{1,0:T(8,128)(2,1)} %param.22) | copy-start | bytes 6291460
  8.0 8.7 %copy-start.10 = (s32[16]{0:T(128)S(1)}, s32[16]{0:T(128)}, u32[]{:S(2)}) copy-start(s32[16]{0:T(128)} %param.16) | copy-start | bytes 196
  8.0 9.3 %copy-start.9 = (s32[16]{0:T(128)S(1)}, s32[16]{0:T(128)}, u32[]{:S(2)}) copy-start(s32[16]{0:T(128)} %param.15) | copy-start | bytes 196
  10.2 21.4 %all-to-all-start = ((bf16[8,32,2048]{2,1,0:T(8,128)(2,1)}), bf16[8,32,2048]{2,1,0:T(8,128)(2,1)S(1)}, u32[]{:S(2)}, u32[]{:S(2)}) async-start(bf16[8,32,2048]{2,1,0:T(8,128)(2,1)} %stack.2), calls=%async_computation | async-start | bytes 2097152 | tf_op jit(solution)/shard_map/all_to_all | solution.py:107
  15.6 98.2 %all-reduce.2.cloned.1.call-start = ((), (), s32[]{:S(2)}) async-start(), calls=%async_computation.3 | async-start | bytes 2097152 | tf_op jit(solution)/shard_map/psum | solution.py:146
  32.5 7.6 %slice-start = ((s8[8388608]{0:T(1024)(128)(4,1)}), s8[4194304]{0:T(1024)(128)(4,1)S(1)}, s32[]{:S(2)}) async-start(s8[8388608]{0:T(1024)(128)(4,1)} %bitcast.91), calls=%async_computation.8 | async-start | bytes 8388608
  32.8 4.4 %copy-start.12 = (bf16[2048,512]{1,0:T(8,128)(2,1)S(1)}, bf16[2048,512]{1,0:T(8,128)(2,1)}, u32[]{:S(2)}) copy-start(bf16[2048,512]{1,0:T(8,128)(2,1)} %param.21) | copy-start | bytes 6291460
  34.7 5.3 %slice-start.1 = ((s8[8388608]{0:T(1024)(128)(4,1)}), s8[4194304]{0:T(1024)(128)(4,1)S(1)}, s32[]{:S(2)}) async-start(s8[8388608]{0:T(1024)(128)(4,1)} %bitcast.91), calls=%async_computation.9 | async-start | bytes 8388608
  37.2 1.6 copy-start.13
  38.8 0.7 copy-start.11
  38.8 1.3 copy-start.7
  40.0 3.7 %copy-start.3 = (bf16[16,16,128]{2,1,0:T(8,128)(2,1)}, bf16[16,16,128]{2,1,0:T(8,128)(2,1)S(1)}, u32[]{:S(2)}) copy-start(bf16[16,16,128]{2,1,0:T(8,128)(2,1)S(1)} %get-tuple-element.10) | copy-start | bytes 196612
  40.0 3.7 %copy-start.4 = (bf16[16,16,128]{2,1,0:T(8,128)(2,1)}, bf16[16,16,128]{2,1,0:T(8,128)(2,1)S(1)}, u32[]{:S(2)}) copy-start(bf16[16,16,128]{2,1,0:T(8,128)(2,1)S(1)} %get-tuple-element.11) | copy-start | bytes 196612
  48.7 3.5 %copy-start.14 = (s32[16]{0:T(128)S(1)}, s32[16]{0:T(128)}, u32[]{:S(2)}) copy-start(s32[16]{0:T(128)} %param.17) | copy-start | bytes 196
  48.7 4.2 %copy-start.5 = (f32[16,16]{1,0:T(8,128)S(1)}, f32[16,16]{1,0:T(8,128)}, u32[]{:S(2)}) copy-start(f32[16,16]{1,0:T(8,128)} %get-tuple-element.16) | copy-start | bytes 3076
  48.7 4.2 %copy-start.6 = (f32[16]{0:T(128)S(1)}, f32[16]{0:T(128)}, u32[]{:S(2)}) copy-start(f32[16]{0:T(128)} %get-tuple-element.13) | copy-start | bytes 196
  50.4 91.8 %all-gather.4.cloned.1.call-start = ((), (), s32[]{:S(2)}) async-start(), calls=%async_computation.4 | async-start | bytes 2228224 | tf_op jit(solution)/shard_map/all_gather | solution.py:152
  51.0 137.9 %all-gather.6.cloned.1.call-start = ((), (), s32[]{:S(2)}) async-start(), calls=%async_computation.5 | async-start | bytes 2228224 | tf_op jit(solution)/shard_map/all_gather | solution.py:157
  51.6 185.9 %all-gather.8.cloned.1.call-start = ((), (), s32[]{:S(2)}) async-start(), calls=%async_computation.6 | async-start | bytes 2228224 | tf_op jit(solution)/shard_map/all_gather | solution.py:163
  61.4 5.1 %copy-start.8 = (pred[16]{0:T(512)(128)(4,1)S(1)}, pred[16]{0:T(512)(128)(4,1)}, u32[]{:S(2)}) copy-start(pred[16]{0:T(512)(128)(4,1)} %compare_and_fusion) | copy-start | bytes 52
  72.1 170.3 %all-to-all-start.1 = ((bf16[16,1,256,512]{3,2,1,0:T(8,128)(2,1)}), bf16[16,1,256,512]{3,2,1,0:T(8,128)(2,1)}, u32[]{:S(2)}, u32[]{:S(2)}) async-start(bf16[16,1,256,512]{3,2,1,0:T(8,128)(2,1)} %fusion.4), calls=%async_computation.2 | async-start | bytes 8388608 | tf_op jit(solution)/shard_map/all_to_all | solution.py:131
  79.1 194.9 %reduce-scatter.2.cloned.1.call-start = ((), (), s32[]{:S(2)}) async-start(), calls=%async_computation.7 | async-start | bytes 1179648 | tf_op jit(solution)/shard_map/reduce_scatter | solution.py:168
  113.8 2.9 %copy-start.1 = (bf16[256,2048]{1,0:T(8,128)(2,1)S(1)}, bf16[256,2048]{1,0:T(8,128)(2,1)}, u32[]{:S(2)}) copy-start(bf16[256,2048]{1,0:T(8,128)(2,1)} %all-reduce.2.cloned.1.call-done) | copy-start | bytes 3145732
  118.7 118.8 %copy-start.2 = (bf16[256,2048]{1,0:T(8,128)(2,1)S(1)}, bf16[256,2048]{1,0:T(8,128)(2,1)}, u32[]{:S(2)}) copy-start(bf16[256,2048]{1,0:T(8,128)(2,1)} %multiply_convert_fusion) | copy-start | bytes 3145732
Sparse Core Ops, SparseCore 0:
  50.5 63.1 all-reduce.1
  242.5 31.5 reduce-scatter.1
Sparse Core Ops, SparseCore 1:
  53.0 89.1 all-gather.3
  144.2 44.7 all-gather.5
  190.9 46.5 all-gather.7
